TPU v7x, 256 devices: a whole 4x4x8 slice. The times are simulated.
256 devices in a mesh: ctx: 16 (over y, x), head: 4 (over z_hi, core), dp: 4 (over z_lo).
Axes of the slice: x: 4, y: 4, z: 8 (z_hi: 2, z_lo: 4; z = z_hi * 4 + z_lo), core: 2. Of those that a mesh axis runs over, the one named last changes fastest.
Arguments:
- queries: bfloat16 [4096, 8, 8, 128], P('ctx', 'head', 'dp'), may hold values from -2.5 to 2.5
- key_rows: bfloat16 [4096, 8, 128], P(('ctx', 'dp'), 'head'), may hold values from -2.5 to 2.5
- value_rows: bfloat16 [4096, 8, 128], P(('ctx', 'dp'), 'head'), may hold values from -6 to 6
- forward_out: bfloat16 [4096, 8, 8, 128], P('ctx', 'head', 'dp'), may hold values from -0.59765625 to 0.59765625
- grad_out: bfloat16 [4096, 8, 8, 128], P('ctx', 'head', 'dp'), may hold values from -24 to 24
- logsumexp: float32 [8, 8, 4096], P('head', 'dp', 'ctx'), as said below
- selected: int32 [16, 8, 8, 8], P('ctx', 'head', 'dp'), may hold values from -1 to 15, as said below
Outputs:
- query_grad: bfloat16 [4096, 8, 8, 128], P('ctx', 'head', 'dp')
- key_grad: float32 [4096, 8, 128], P(('ctx', 'dp'), 'head')
- value_grad: float32 [4096, 8, 128], P(('ctx', 'dp'), 'head')
Inputs may be any that keep to these rules, and one draw needn't show every extreme that they name: selected[i, a, g, 0] = i. The other entries of a row are distinct blocks below i (some blocks below i may be left out), followed by -1 in the slots that remain. `logsumexp`: each entry lies between log(512) and log(512) + 1.5.
All inputs are finite; a program needn't handle non-finite values.
Results may differ from a plain program's by a relative error of at most 0.0051.
Values may be sent and summed in bfloat16 or wider, within the bound.
No kernel may reach another device: no remote copies, remote signals or barrier semaphores. Data moves between devices by JAX's collectives and lax.ppermute only.
A program may use at most 64 MiB of HBM per device.

v0:
```python
import jax
import jax.numpy as jnp
from jax import lax
from jax.sharding import PartitionSpec as P

BLOCK = 256


def block_terms(
    query_blk,
    grad_blk,
    lse_row,
    delta_part,
    slot_ids,
    key_view,
    value_layout,
    head_local,
    slot_offset,
    softmax_scale,
):
    slot_count = slot_ids.shape[0]
    block_len = query_blk.shape[0]
    safe_ids = jnp.maximum(slot_ids, 0)
    positions = jnp.arange(block_len, dtype=jnp.int32)
    key_sel = key_view[safe_ids[:, None], positions[None, :], head_local].reshape(
        slot_count * block_len, -1
    )
    value_sel = value_layout[safe_ids[:, None], positions[None, :], head_local].reshape(
        slot_count * block_len, -1
    )
    columns = jnp.arange(slot_count * block_len, dtype=jnp.int32)
    slot_of = columns // block_len
    within = columns % block_len
    filled = slot_ids[slot_of] >= 0
    causal = (slot_of + slot_offset != 0)[None, :] | (within[None, :] <= positions[:, None])
    keep = filled[None, :] & causal
    score_rows = (
        lax.dot_general(
            query_blk, key_sel, (((1,), (1,)), ((), ())), preferred_element_type=jnp.float32
        )
        * softmax_scale
    )
    probs = jnp.where(keep, jnp.exp(score_rows - lse_row[:, None]), jnp.float32(0.0))
    probs_low = probs.astype(jnp.bfloat16)
    value_part = lax.dot_general(
        probs_low, grad_blk, (((0,), (0,)), ((), ())), preferred_element_type=jnp.float32
    )
    dprobs = lax.dot_general(
        grad_blk, value_sel, (((1,), (1,)), ((), ())), preferred_element_type=jnp.float32
    )
    dscores = (probs * (dprobs - delta_part[:, None]) * softmax_scale).astype(jnp.bfloat16)
    query_part = jnp.dot(dscores, key_sel, preferred_element_type=jnp.float32)
    key_part = lax.dot_general(
        dscores, query_blk, (((0,), (0,)), ((), ())), preferred_element_type=jnp.float32
    )
    return (
        query_part,
        key_part.reshape(slot_count, block_len, -1),
        value_part.reshape(slot_count, block_len, -1),
    )


def local(queries, key_rows, value_rows, forward_out, grad_out, logsumexp, selected):
    rows_local, kv_local, group_local, head_dim = queries.shape
    blocks_local = selected.shape[0]
    slot_total = selected.shape[3]
    half_slots = slot_total // 2
    softmax_scale = head_dim ** (-0.5)
    keys_all, values_all = (
        lax.all_gather(key_rows, ("ctx", "dp"), axis=0, tiled=True),
        lax.all_gather(value_rows, ("ctx", "dp"), axis=0, tiled=True),
    )
    total_rows = keys_all.shape[0]
    block_total = total_rows // BLOCK
    key_view = keys_all.reshape(block_total, BLOCK, kv_local, head_dim)
    value_layout = values_all.reshape(block_total, BLOCK, kv_local, head_dim)
    positions = jnp.arange(BLOCK, dtype=jnp.int32)
    delta_rows = jnp.sum(grad_out.astype(jnp.float32) * forward_out.astype(jnp.float32), axis=-1)

    def head_step(carried, item_index):
        key_acc, value_acc = carried
        block_index = item_index // (kv_local * group_local)
        head_local = item_index // group_local % kv_local
        group_index = item_index % group_local
        zero_index = jnp.zeros((), jnp.int32)
        row_start = block_index * BLOCK
        query_blk = lax.dynamic_slice(
            queries, (row_start, head_local, group_index, zero_index), (BLOCK, 1, 1, head_dim)
        ).reshape(BLOCK, head_dim)
        grad_blk = lax.dynamic_slice(
            grad_out, (row_start, head_local, group_index, zero_index), (BLOCK, 1, 1, head_dim)
        ).reshape(BLOCK, head_dim)
        lse_row = lax.dynamic_slice(
            logsumexp, (head_local, group_index, row_start), (1, 1, BLOCK)
        ).reshape(BLOCK)
        delta_part = lax.dynamic_slice(
            delta_rows, (row_start, head_local, group_index), (BLOCK, 1, 1)
        ).reshape(BLOCK)
        slot_ids = lax.dynamic_slice(
            selected, (block_index, head_local, group_index, zero_index), (1, 1, 1, slot_total)
        ).reshape(slot_total)
        query_acc = jnp.zeros((BLOCK, head_dim), jnp.float32)
        for half_index in range(2):
            offset = half_index * half_slots
            part_ids = slot_ids[offset : offset + half_slots]
            query_part, key_part, value_part = block_terms(
                query_blk,
                grad_blk,
                lse_row,
                delta_part,
                part_ids,
                key_view,
                value_layout,
                head_local,
                offset,
                softmax_scale,
            )
            target_ids = jnp.where(part_ids >= 0, part_ids, block_total)
            key_acc = key_acc.at[target_ids[:, None], positions[None, :], head_local].add(
                key_part, mode="drop"
            )
            value_acc = value_acc.at[target_ids[:, None], positions[None, :], head_local].add(
                value_part, mode="drop"
            )
            query_acc = query_acc + query_part
        return ((key_acc, value_acc), query_acc.astype(jnp.bfloat16))

    empty = jnp.zeros((block_total, BLOCK, kv_local, head_dim), jnp.float32)
    items = jnp.arange(blocks_local * kv_local * group_local, dtype=jnp.int32)
    (key_acc, value_acc), query_blocks = lax.scan(head_step, (empty, empty), items)
    query_grad = (
        query_blocks.reshape(blocks_local, kv_local, group_local, BLOCK, head_dim)
        .transpose(0, 3, 1, 2, 4)
        .reshape(rows_local, kv_local, group_local, head_dim)
    )
    key_terms = key_acc.reshape(total_rows, kv_local, head_dim)
    value_terms = value_acc.reshape(total_rows, kv_local, head_dim)
    key_grad, value_grad = (
        lax.psum_scatter(key_terms, ("ctx", "dp"), scatter_dimension=0, tiled=True),
        lax.psum_scatter(value_terms, ("ctx", "dp"), scatter_dimension=0, tiled=True),
    )
    return (query_grad, key_grad, value_grad)


def solution(mesh):
    return jax.shard_map(
        local,
        mesh=mesh,
        in_specs=(
            P("ctx", "head", "dp", None),
            P(("ctx", "dp"), "head", None),
            P(("ctx", "dp"), "head", None),
            P("ctx", "head", "dp", None),
            P("ctx", "head", "dp", None),
            P("head", "dp", "ctx"),
            P("ctx", "head", "dp", None),
        ),
        out_specs=(
            P("ctx", "head", "dp", None),
            P(("ctx", "dp"), "head", None),
            P(("ctx", "dp"), "head", None),
        ),
        check_vma=False,
    )
```

profile of v0, /device:TPU:0, one launch (start us, length us, event | category | flops | bytes accessed | tf_op | source)
XLA Modules:
  0.0 1941.0 jit_solution(5706698245401311569)
XLA Ops:
  14.0 347.1 %all-gather.3.cloned.1.call-done = bf16[4096,2,128]{2,1,0:T(2,128)(2,1)} async-done(((bf16[64,2,128]{2,1,0:T(2,128)(2,1)}), bf16[4096,2,128]{2,1,0:T(2,128)(2,1)}) %all-gather.3.cloned.1.call-update) | async-done | bytes 2097168 | tf_op jit(solution)/shard_map/all_gather | solution.py:70
  361.1 349.4 %all-gather.5.cloned.1.call-done = bf16[4096,2,128]{2,1,0:T(2,128)(2,1)} async-done(((bf16[64,2,128]{2,1,0:T(2,128)(2,1)}), bf16[4096,2,128]{2,1,0:T(2,128)(2,1)}) %all-gather.5.cloned.1.call-update) | async-done | bytes 2097168 | tf_op jit(solution)/shard_map/all_gather | solution.py:71
  717.9 441.2 %while.19 = (s32[]{:T(128)}, f32[16,256,2,128]{3,2,1,0:T(2,128)}, f32[16,256,2,128]{3,2,1,0:T(2,128)}, bf16[4,256,128]{2,1,0:T(8,128)(2,1)}, s32[4]{0:T(128)S(1)...) while((s32[]{:T(128)}, f32[16,256,2,128]{3,2,1,0:T(2,128)}, ...), condition=%wide.region_6.7_spmd.clone.clone, body=%wide.region_1.6_spmd.clone.clone.sunk | while | flops 682269824 | bytes 35151920 | solution.py:130
  735.1 12.7 gather_fusion.3
  747.7 6.2 gather_fusion
  753.9 12.7 gather_fusion.2
  789.4 10.0 scatter_fusion.2
  799.4 10.0 scatter_fusion.3
  809.3 9.5 scatter_fusion
  818.8 9.5 scatter_fusion.1
  845.3 12.7 gather_fusion.3
  858.0 6.2 gather_fusion
  864.1 12.7 gather_fusion.2
  899.6 10.0 scatter_fusion.2
  909.6 10.0 scatter_fusion.3
  919.6 9.5 scatter_fusion
  929.1 9.5 scatter_fusion.1
  955.6 12.7 gather_fusion.3
  968.2 6.2 gather_fusion
  974.4 12.7 gather_fusion.2
  1009.9 10.0 scatter_fusion.2
  1019.9 10.0 scatter_fusion.3
  1029.8 9.5 scatter_fusion
  1039.3 9.5 scatter_fusion.1
  1065.8 12.7 gather_fusion.3
  1078.5 6.2 gather_fusion
  1084.6 12.7 gather_fusion.2
  1120.1 10.0 scatter_fusion.2
  1130.1 10.0 scatter_fusion.3
  1140.1 9.5 scatter_fusion
  1149.6 9.5 scatter_fusion.1
  1161.9 771.0 %all-reduce.5.cloned.1.call-done = (f32[4096,2,128]{2,1,0:T(2,128)}, f32[4096,2,128]{2,1,0:T(2,128)}) async-done(((f32[4096,2,128]{2,1,0:T(2,128)}, f32[4096,2,128]{2,1,0:T(2,128)}), (f32[4096,2,128]{2,1,0:T(2,128)}, f32[4096,2,128]{2,1,0:T(2,128)})) %all-reduce.5.cloned.1.call-update) | async-done | bytes 8388624
  (179 shorter events, 166.1 us)
Async XLA Ops:
  7.2 354.0 %all-gather.3.cloned.1.call-start = ((), (), s32[]{:S(2)}) async-start(), calls=%async_computation | async-start | bytes 2129920 | tf_op jit(solution)/shard_map/all_gather | solution.py:70
  7.9 702.6 %all-gather.5.cloned.1.call-start = ((), (), s32[]{:S(2)}) async-start(), calls=%async_computation.1 | async-start | bytes 2129920 | tf_op jit(solution)/shard_map/all_gather | solution.py:71
  8.6 1924.3 %all-reduce.5.cloned.1.call-start = ((), (), s32[]{:S(2)}) async-start(), calls=%async_computation.2 | async-start | bytes 16777216
  710.5 7.4 copy-start
  710.5 7.4 copy-start.3
  710.5 7.4 copy-start.4
  774.2 6.5 copy-start.1
  884.4 6.5 copy-start.1
  994.7 6.5 copy-start.1
  1104.9 6.5 copy-start.1
  1159.1 0.7 copy-start.5
  1159.1 1.9 copy-start.2
Sparse Core Ops, SparseCore 0:
  9.8 351.3 all-gather.2
  362.9 347.5 all-gather.4
  1159.3 773.6 all-reduce.4
where the time goes:
time: 1950 us; the launch traced here: 1940 us
  waiting for transfers between devices  1470 us (75%)
  local copies, waits for them, and re-layouts  205 us (11%)
  other arithmetic  179 us (9%)
  matrix products  62.6 us (3%)
    unnamed x4, waiting for transfers between devices  772 us
    all_gather x1, waiting for transfers between devices, local(): lax.all_gather(value_rows, ('ctx', 'dp'), axis=0, tiled=True)  349 us
    all_gather x1, waiting for transfers between devices, local(): lax.all_gather(key_rows, ('ctx', 'dp'), axis=0, tiled=True)  347 us
    while x32, other arithmetic  157 us
    gather x8, local copies, waits for them, and re-layouts, block_terms(): value_layout[safe_ids[:, None], positions[None, :], head_local]  101 us
    gather x8, local copies, waits for them, and re-layouts, block_terms(): key_view[safe_ids[:, None], positions[None, :], head_local]  49.2 us
  transfers between devices with their start and end apart: 3, of which 3 were waited for; matrix products, arithmetic and copies ran while one was open for 0% of the time, Pallas kernels for 0%

commit v1 on v0

--- a/solution.py
+++ b/solution.py
@@ -4,6 +4,11 @@
 from jax.sharding import PartitionSpec as P
 
 BLOCK = 256
+
+
+def gather_over(array, axis, along):
+    repeated = jnp.stack([array] * lax.axis_size(axis))
+    return jnp.concatenate(lax.all_to_all(repeated, axis, 0, 0), axis=along)
 
 
 def block_terms(
@@ -67,7 +72,7 @@
     half_slots = slot_total // 2
     softmax_scale = head_dim ** (-0.5)
     keys_all, values_all = (
-        lax.all_gather(key_rows, ("ctx", "dp"), axis=0, tiled=True),
+        gather_over(key_rows, ("ctx", "dp"), 0),
         lax.all_gather(value_rows, ("ctx", "dp"), axis=0, tiled=True),
     )
     total_rows = keys_all.shape[0]

time: 1950 us -> 1600 us (0.82)
  waiting for transfers between devices: 1470 us -> 1110 us
    all_gather x1 -> x0, waiting for transfers between devices: 347 us -> none  [local(): lax.all_gather(key_rows, ('ctx', 'dp'), axis=0, tiled=True)]
    unnamed x4 -> x3, waiting for transfers between devices: 772 us -> 772 us
  transfers between devices with their start and end apart: 3 -> 3, of which waited for: 3 -> 2; matrix products, arithmetic and copies ran while one was open for 0% -> 1% of each run, Pallas kernels for 0% -> 0%
where the time goes in v1:
time: 1600 us; the launch traced here: 1590 us
  waiting for transfers between devices  1110 us (69%)
  local copies, waits for them, and re-layouts  207 us (13%)
  other arithmetic  178 us (11%)
  matrix products  62.4 us (4%)
    unnamed x3, waiting for transfers between devices  772 us
    all_gather x1, waiting for transfers between devices, local(): lax.all_gather(value_rows, ('ctx', 'dp'), axis=0, tiled=True)  338 us
    while x32, other arithmetic  157 us
    gather x8, local copies, waits for them, and re-layouts, block_terms(): value_layout[safe_ids[:, None], positions[None, :], head_local]  101 us
    gather x8, local copies, waits for them, and re-layouts, block_terms(): key_view[safe_ids[:, None], positions[None, :], head_local]  49.2 us
  transfers between devices with their start and end apart: 3, of which 2 were waited for; matrix products, arithmetic and copies ran while one was open for 1% of the time, Pallas kernels for 0%

profile of v1, /device:TPU:0, one launch (start us, length us, event | category | flops | bytes accessed | tf_op | source)
XLA Modules:
  0.0 1593.8 jit_solution(10469738694188776644)
XLA Ops:
  12.0 10.3 all-to-all-start
  24.8 338.1 %all-gather.2.cloned.1.call-done = bf16[4096,2,128]{2,1,0:T(2,128)(2,1)} async-done(((bf16[64,2,128]{2,1,0:T(2,128)(2,1)}), bf16[4096,2,128]{2,1,0:T(2,128)(2,1)}) %all-gather.2.cloned.1.call-update) | async-done | bytes 2097168 | tf_op jit(solution)/shard_map/all_gather | solution.py:76
  370.4 440.5 %while.19 = (s32[]{:T(128)}, f32[16,256,2,128]{3,2,1,0:T(2,128)}, f32[16,256,2,128]{3,2,1,0:T(2,128)}, bf16[4,256,128]{2,1,0:T(8,128)(2,1)}, s32[4]{0:T(128)S(1)...) while((s32[]{:T(128)}, f32[16,256,2,128]{3,2,1,0:T(2,128)}, ...), condition=%wide.region_6.7_spmd.clone.clone, body=%wide.region_1.6_spmd.clone.clone.sunk | while | flops 682269824 | bytes 35151920 | solution.py:135
  387.4 12.6 gather_fusion.3
  400.0 6.2 gather_fusion
  406.1 12.6 gather_fusion.2
  441.5 10.0 scatter_fusion.2
  451.4 10.0 scatter_fusion.3
  461.4 9.6 scatter_fusion
  471.0 9.6 scatter_fusion.1
  497.5 12.6 gather_fusion.3
  510.1 6.2 gather_fusion
  516.2 12.6 gather_fusion.2
  551.6 10.0 scatter_fusion.2
  561.6 10.0 scatter_fusion.3
  571.5 9.6 scatter_fusion
  581.1 9.6 scatter_fusion.1
  607.6 12.6 gather_fusion.3
  620.2 6.2 gather_fusion
  626.4 12.6 gather_fusion.2
  661.7 10.0 scatter_fusion.2
  671.7 10.0 scatter_fusion.3
  681.6 9.6 scatter_fusion
  691.2 9.6 scatter_fusion.1
  717.7 12.6 gather_fusion.3
  730.3 6.2 gather_fusion
  736.5 12.6 gather_fusion.2
  771.8 10.0 scatter_fusion.2
  781.8 10.0 scatter_fusion.3
  791.7 9.6 scatter_fusion
  801.3 9.6 scatter_fusion.1
  813.7 771.7 %all-reduce.5.cloned.1.call-done = (f32[4096,2,128]{2,1,0:T(2,128)}, f32[4096,2,128]{2,1,0:T(2,128)}) async-done(((f32[4096,2,128]{2,1,0:T(2,128)}, f32[4096,2,128]{2,1,0:T(2,128)}), (f32[4096,2,128]{2,1,0:T(2,128)}, f32[4096,2,128]{2,1,0:T(2,128)})) %all-reduce.5.cloned.1.call-update) | async-done | bytes 8388624
  (183 shorter events, 166.4 us)
Async XLA Ops:
  7.2 15.2 copy-start.3
  7.2 15.9 copy-start.1
  7.2 16.7 %copy-start.2 = (bf16[256,2,2,128]{3,2,1,0:T(2,128)(2,1)S(1)}, bf16[256,2,2,128]{3,2,1,0:T(2,128)(2,1)}, u32[]{:S(2)}) copy-start(bf16[256,2,2,128]{3,2,1,0:T(2,128)(2,1)} %param.12) | copy-start | bytes 786436
  7.2 355.8 %all-gather.2.cloned.1.call-start = ((), (), s32[]{:S(2)}) async-start(), calls=%async_computation.1 | async-start | bytes 2129920 | tf_op jit(solution)/shard_map/all_gather | solution.py:76
  12.0 351.0 %all-to-all-start = ((bf16[64,64,2,128]{3,2,1,0:T(2,128)(2,1)}), bf16[64,64,2,128]{3,2,1,0:T(2,128)(2,1)S(1)}, u32[]{:S(2)}, u32[]{:S(2)}) async-start(bf16[64,64,2,128]{3,2,1,0:T(2,128)(2,1)} %stack.2), calls=%async_computation | async-start | bytes 4194304 | tf_op jit(solution)/shard_map/all_to_all | solution.py:11
  22.3 1563.1 %all-reduce.5.cloned.1.call-start = ((), (), s32[]{:S(2)}) async-start(), calls=%async_computation.2 | async-start | bytes 16777216
  363.0 7.4 copy-start.5
  363.0 7.4 copy-start.6
  426.3 6.5 copy-start
  536.4 6.5 copy-start
  646.5 6.5 copy-start
  756.7 6.5 copy-start
  810.9 0.7 copy-start.7
  810.9 1.9 copy-start.4
Sparse Core Ops, SparseCore 0:
  9.8 353.1 all-gather.1
  811.0 774.3 all-reduce.4
